TPU v7x, 128 devices: a whole 4x4x4 slice. The times are simulated.
128 devices in a mesh: tiles: 16 (over y, z), nests: 8 (over x, core).
Axes of the slice: x: 4, y: 4, z: 4, core: 2. Of those that a mesh axis runs over, the one named last changes fastest.
Arguments:
- parent: float32 [1024, 2048, 128], P('tiles', 'nests'), may hold values from -6 to 6
- nest_state: float32 [8, 64, 128, 128], P('nests', 'tiles'), may hold values from -6 to 6
- parent_mix: float32 [128, 128], replicated, may hold values from -0.24 to 0.24
- nest_mix: float32 [128, 128], replicated, may hold values from -0.24 to 0.24
- courant: float32 [2, 128], replicated, may hold values from 0.05 to 0.45
- nest_pos: int32 [8, 2], P('nests'), may hold values from 0 to 5954, as said below
Outputs:
- parent_out: float32 [1024, 2048, 128], P('tiles', 'nests')
- nest_out: float32 [8, 64, 128, 128], P('nests', 'tiles')
Inputs may be any that keep to these rules, and one draw needn't show every extreme that they name: nest_pos[n] = (3 i + a, 3 q + c) with a, c in 0..2, i <= 1001, and n * 256 <= q <= (n + 1) * 256 - 64: nest n reads and feeds only parent columns of the n-th group of 256 columns.
All inputs are finite; a program needn't handle non-finite values.
Results may differ from a plain program's by a relative error of at most 0.0003.
Values sent between devices are 32-bit elements; how exact they have to be, the bound alone decides.
No kernel may reach another device: no remote copies, remote signals or barrier semaphores. Data moves between devices by JAX's collectives and lax.ppermute only.
A program may use at most 128 MiB of HBM per device.

v0:
```python
import jax
import jax.numpy as jnp
from jax import lax
from jax.sharding import PartitionSpec as P

BLK = 64
STEPS = 3
KAPPA = 0.125
HIGH = lax.Precision.HIGHEST


def with_halo(block, sides, width):
    for axis, dim in sides:
        count = lax.axis_size(axis)
        forward = [(i, i + 1) for i in range(count - 1)]
        backward = [(target, source) for source, target in forward]
        low = lax.ppermute(
            lax.slice_in_dim(block, block.shape[dim] - width, None, axis=dim), axis, forward
        )
        high = lax.ppermute(lax.slice_in_dim(block, 0, width, axis=dim), axis, backward)
        block = jnp.concatenate([low, block, high], axis=dim)
    return block


def passed_along(block, axis, distance):
    devices = range(lax.axis_size(axis))
    route = [(i - distance, i) for i in devices if i - distance in devices]
    return lax.ppermute(block, axis, route)


def nest_advance(current, upper, edge, courant, nest_mix):
    left = jnp.concatenate([edge, current[:, :-1]], axis=1)
    mixed = jnp.einsum("xyc,cd->xyd", current, nest_mix, precision=HIGH)
    return current + courant[0] * (upper - current) + courant[1] * (left - current) + mixed


def bilinear(data, anchor, rows, columns_count, block_len):
    cols = jnp.arange(columns_count, dtype=jnp.int32)
    spot = anchor[1] + cols
    near = spot // 3 - anchor[1] // 3
    frac_y = (spot % 3).astype(jnp.float32) / 3.0
    places = jnp.arange(block_len, dtype=jnp.int32)[None, :]
    zero = jnp.zeros((columns_count, block_len), jnp.float32)
    table = jnp.where(places == near[:, None], (1.0 - frac_y)[:, None] + zero, zero)
    table = table + jnp.where(places == near[:, None] + 1, frac_y[:, None] + zero, zero)
    frac_x = ((anchor[0] + rows) % 3).astype(jnp.float32) / 3.0
    upper_part = jnp.einsum("nb,xbc->xnc", table, data[:, 0], precision=HIGH)
    lower_part = jnp.einsum("nb,xbc->xnc", table, data[:, 1], precision=HIGH)
    return (1.0 - frac_x)[:, None, None] * upper_part + frac_x[:, None, None] * lower_part


def shards(parent, nest_state, parent_mix, nest_mix, courant, nest_pos):
    tile_rows, tile_cols, width = parent.shape
    nest_rows = nest_state.shape[1]
    nest_cols = nest_state.shape[2]
    tiles_count = lax.axis_size("tiles")
    slots = (nest_rows + 1) // 3 + 2
    tile_index = lax.axis_index("tiles")
    column_index = lax.axis_index("nests")
    anchor = nest_pos[0]
    corner = anchor[1] // 3
    base = tile_index * nest_rows
    lowest = (anchor[0] + base) // 3
    strip = lax.dynamic_slice_in_dim(parent, corner - column_index * tile_cols, BLK, 1)
    receivers = jnp.arange(tiles_count, dtype=jnp.int32)
    wanted = ((anchor[0] + receivers * nest_rows) // 3)[:, None] + jnp.arange(
        slots, dtype=jnp.int32
    )[None, :]
    local = wanted - tile_index * tile_rows
    inside = (local >= 0) & (local < tile_rows)
    taken = strip[jnp.clip(local, 0, tile_rows - 1)]
    local_rows = lax.psum_scatter(
        jnp.where(inside[..., None, None], taken, 0.0), "tiles", scatter_dimension=0, tiled=True
    ).reshape(slots, BLK, width)
    padded = with_halo(parent, (("tiles", 0), ("nests", 1)), 1)
    beside_all = padded[2:, 1:-1] + padded[:-2, 1:-1] + padded[1:-1, 2:] + padded[1:-1, :-2]
    mixed = jnp.einsum("xyc,cd->xyd", parent, parent_mix, precision=HIGH)
    parent_new = parent + KAPPA * (beside_all - 4.0 * parent) + mixed
    rows = base + jnp.arange(nest_rows, dtype=jnp.int32)
    near_row = (anchor[0] + rows) // 3 - lowest
    data = jnp.stack([local_rows[near_row], local_rows[near_row + 1]], axis=1)
    interp = bilinear(data, anchor, rows, nest_cols, BLK)
    start = 0.5 * (nest_state[0] + interp)
    first = tile_index == 0
    edge = start[:, :1]
    current = start
    for step in range(STEPS):
        above = passed_along(current[-1:], "tiles", 1)
        above = jnp.where(first, start[:1], above)
        upper = jnp.concatenate([above, current[:-1]], axis=0)
        current = nest_advance(current, upper, edge, courant, nest_mix)
    fb_rows = (nest_rows + 2) // 3
    fb_cols = (nest_cols + 2) // 3
    counter = jnp.arange(fb_rows, dtype=jnp.int32)
    ys = -anchor[1] % 3 + 3 * jnp.arange(fb_cols, dtype=jnp.int32)
    col_live = ys < nest_cols
    xs = base + -(anchor[0] + base) % 3 + 3 * counter
    row_live = xs < base + nest_rows
    own_values = current[jnp.clip(xs - base, 0, nest_rows - 1)][:, jnp.clip(ys, 0, nest_cols - 1)]
    own_values = jnp.where((row_live[:, None] & col_live[None, :])[..., None], own_values, 0.0)
    pcol = (anchor[1] + ys) // 3 - column_index * tile_cols
    col_ok = col_live & (pcol >= 0) & (pcol < tile_cols)
    piece = lax.all_gather(own_values, "tiles", axis=0, tiled=True)
    slot_index = jnp.arange(piece.shape[0], dtype=jnp.int32)
    sender = slot_index // fb_rows
    sender_base = sender * nest_rows
    sender_x = sender_base + -(anchor[0] + sender_base) % 3 + 3 * (slot_index % fb_rows)
    prow = (anchor[0] + sender_x) // 3 - tile_index * tile_rows
    row_ok = (sender_x < sender_base + nest_rows) & (prow >= 0) & (prow < tile_rows)
    valid = row_ok[:, None] & col_ok[None, :]
    old = parent_new[
        jnp.clip(prow, 0, tile_rows - 1)[:, None], jnp.clip(pcol, 0, tile_cols - 1)[None, :]
    ]
    diff = jnp.where(valid[..., None], 0.5 * (piece - old), 0.0)
    row_index = jnp.where(valid, prow[:, None], tile_rows)
    col_index = jnp.broadcast_to(jnp.clip(pcol, 0, tile_cols - 1)[None, :], valid.shape)
    parent_out = parent_new.at[row_index, col_index].add(diff, mode="drop")
    return (parent_out, current[None])


def solution(mesh):
    placed = (
        P("tiles", "nests", None),
        P("nests", "tiles", None, None),
        P(),
        P(),
        P(),
        P("nests", None),
    )
    return jax.shard_map(
        shards,
        mesh=mesh,
        in_specs=placed,
        out_specs=(P("tiles", "nests", None), P("nests", "tiles", None, None)),
        check_vma=False,
    )
```

profile of v0, /device:TPU:6, one launch (start us, length us, event | category | flops | bytes accessed | tf_op | source)
XLA Modules:
  0.0 216.7 jit_solution(3485163505775321891)
XLA Ops:
  7.3 1.0 fusion.71
  8.3 3.8 %collective-permute-start.1 = (f32[1,256,128]{2,1,0:T(8,128)S(1)}, f32[1,256,128]{2,1,0:T(8,128)S(1)}, u32[]{:S(2)}, u32[]{:S(2)}) collective-permute-start(f32[1,256,128]{2,1,0:T(8,128)S(1)} %get-tuple-element.13), channel_id=1, source_target_pairs={{0,8},{8,16},{16,24},{24,32},{32,40},{40,48},{48,56},{56,64},{64,7... | collective-permute-start | bytes 393224 | tf_op jit(solution)/shard_map/ppermute | solution.py:17
  12.1 1.3 collective-permute-start
  13.4 1.3 fusion.72
  18.1 2.0 constant_dynamic-slice_fusion
  20.3 1.8 gather_fusion
  22.0 2.7 %broadcast_select_fusion = f32[16,3,64,128]{3,2,1,0:T(8,128)} fusion(f32[16,3,64,128]{3,2,1,0:T(8,128)} %bitcast.60, pred[16,3]{1,0:T(8,128)(4,1)S(1)} %fusion.44), kind=kLoop, calls=%fused_computation.28 | loop fusion | flops 393216 | bytes 3145776 | tf_op jit(solution)/shard_map/jit(_where)/select_n | solution.py:73
  25.5 0.7 fusion.58
  30.2 0.7 compare_and_fusion.1
  32.3 7.7 %constant_dynamic-update-slice_fusion.1 = f32[66,256,128]{2,1,0:T(8,128)} fusion(f32[66,256,128]{2,1,0:T(8,128)} %constant_dynamic-update-slice_fusion.2, f32[64,256,128]{2,1,0:T(8,128)} %param.6), kind=kLoop, calls=%fused_computation.88 | loop fusion | bytes 16777216
  40.0 61.8 %reduce-scatter.4.cloned.1.call-done = f32[1,3,64,128]{3,2,1,0:T(8,128)} async-done(((f32[16,3,64,128]{3,2,1,0:T(8,128)}), f32[1,3,64,128]{3,2,1,0:T(8,128)}) %reduce-scatter.4.cloned.1.call-update) | async-done | bytes 98320
  101.8 1.4 gather_fusion.1
  103.2 1.4 gather_fusion.2
  105.6 3.1 %collective-permute-start.4 = (f32[1,128,128]{2,1,0:T(8,128)S(1)}, f32[1,128,128]{2,1,0:T(8,128)S(1)}, u32[]{:S(2)}, u32[]{:S(2)}) collective-permute-start(f32[1,128,128]{2,1,0:T(8,128)S(1)} %slice.129), channel_id=1, source_target_pairs={{0,8},{8,16},{16,24},{24,32},{32,40},{40,48},{48,56},{56,64},{64,7... | collective-permute-start | bytes 196616 | tf_op jit(solution)/shard_map/ppermute | solution.py:28
  109.4 1.2 collective-permute-done.4
  111.0 4.3 %collective-permute-start.5 = (f32[1,128,128]{2,1,0:T(8,128)S(1)}, f32[1,128,128]{2,1,0:T(8,128)S(1)}, u32[]{:S(2)}, u32[]{:S(2)}) collective-permute-start(f32[1,128,128]{2,1,0:T(8,128)S(1)} %slice.133), channel_id=1, source_target_pairs={{0,8},{8,16},{16,24},{24,32},{32,40},{40,48},{48,56},{56,64},{64,7... | collective-permute-start | bytes 196616 | tf_op jit(solution)/shard_map/ppermute | solution.py:28
  115.3 1.1 fusion.70
  116.3 1.9 collective-permute-start.3
  118.3 3.6 %collective-permute-start.2 = (f32[66,1,128]{2,1,0:T(1,128)S(1)}, f32[66,1,128]{2,1,0:T(1,128)S(1)}, u32[]{:S(2)}, u32[]{:S(2)}) collective-permute-start(f32[66,1,128]{2,1,0:T(1,128)S(1)} %get-tuple-element.10), channel_id=1, source_target_pairs={{1,0},{2,1},{3,2},{4,3},{5,4},{6,5},{7,6},{9,8},{10,9},{11,10},{12... | collective-permute-start | bytes 101384 | tf_op jit(solution)/shard_map/ppermute | solution.py:20
  122.4 3.3 %collective-permute-start.6 = (f32[1,128,128]{2,1,0:T(8,128)S(1)}, f32[1,128,128]{2,1,0:T(8,128)S(1)}, u32[]{:S(2)}, u32[]{:S(2)}) collective-permute-start(f32[1,128,128]{2,1,0:T(8,128)S(1)} %slice.136), channel_id=1, source_target_pairs={{0,8},{8,16},{16,24},{24,32},{32,40},{40,48},{48,56},{56,64},{64,7... | collective-permute-start | bytes 196616 | tf_op jit(solution)/shard_map/ppermute | solution.py:28
  125.7 27.0 %fusion.4 = f32[64,256,128]{2,1,0:T(8,128)} fusion(f32[64,256,128]{2,1,0:T(8,128)} %param.6, f32[66,256,128]{2,1,0:T(8,128)} %constant_dynamic-update-slice_fusion, f32[66,1,128]{2,1,0:T(1,128)S(1)} %collective-permute-done.3, f32[66,1,128]{2,1,0:T(1,128)S(1)} %collective-permute-done.2, f32[1,256,128]{2,1,0:T(8,128)S(1)} %collective-permute-done.1, ...), kind=kOutput, calls=%fused_computation.12 | convolution fusion | flops 3246391296 | bytes 25823232 | tf_op jit(solution)/shard_map/xyc,cd->xyd/dot_general | solution.py:77
  152.7 14.5 %gather_fusion.5 = f32[1376,128]{1,0:T(8,128)S(1)} fusion(f32[64,256,128]{2,1,0:T(8,128)} %fusion.4, s32[1376]{0:T(1024)S(1)} %reshape.571), kind=kCustom, calls=%fused_computation.5 | custom fusion | bytes 1420032 | tf_op jit(solution)/shard_map/gather | solution.py:111
  169.2 25.4 %all_gather.3 = f32[32,43,128]{2,1,0:T(8,128)S(1)} all-gather(f32[2,43,128]{2,1,0:T(8,128)S(1)} %copy.12), channel_id=1, replica_groups=mesh['tiles'=16,'nests'=8] {'tiles'}, dimensions={0}, use_global_device_ids=true | all-gather | bytes 748544 | tf_op jit(solution)/shard_map/all_gather | solution.py:103
  195.0 14.9 %scatter_fusion = f32[16384,128]{1,0:T(8,128)} fusion(f32[16384,128]{1,0:T(8,128)} %bitcast.58, s32[1376]{0:T(1024)S(1)} %reshape.577, f32[1376,128]{1,0:T(8,128)S(1)} %reshape.579), kind=kCustom, calls=%fused_computation.6 | custom fusion | flops 176128 | bytes 2119040
  (78 shorter events, 10.9 us)
Async XLA Ops:
  7.2 118.5 %copy-start = (f32[128,128]{1,0:T(8,128)S(1)}, f32[128,128]{1,0:T(8,128)}, u32[]{:S(2)}) copy-start(f32[128,128]{1,0:T(8,128)} %param.8) | copy-start | bytes 196612
  7.2 23.8 %copy-start.6 = (s32[2]{0:T(128)S(1)}, s32[2]{0:T(128)}, u32[]{:S(2)}) copy-start(s32[2]{0:T(128)} %constant.162) | copy-start | bytes 28
  7.2 23.9 %copy-start.5 = (s32[2]{0:T(128)S(1)}, s32[2]{0:T(128)}, u32[]{:S(2)}) copy-start(s32[2]{0:T(128)} %constant.165) | copy-start | bytes 28
  7.2 23.9 %copy-start.4 = (f32[2,128]{1,0:T(2,128)S(1)}, f32[2,128]{1,0:T(2,128)}, u32[]{:S(2)}) copy-start(f32[2,128]{1,0:T(2,128)} %param.10) | copy-start | bytes 3076
  7.2 94.6 %reduce-scatter.4.cloned.1.call-start = ((), (), s32[]{:S(2)}) async-start(), calls=%async_computation.1 | async-start | bytes 1671168
  8.3 23.4 %collective-permute-start.1 = (f32[1,256,128]{2,1,0:T(8,128)S(1)}, f32[1,256,128]{2,1,0:T(8,128)S(1)}, u32[]{:S(2)}, u32[]{:S(2)}) collective-permute-start(f32[1,256,128]{2,1,0:T(8,128)S(1)} %get-tuple-element.13), channel_id=1, source_target_pairs={{0,8},{8,16},{16,24},{24,32},{32,40},{40,48},{48,56},{56,64},{64,7... | collective-permute-start | bytes 393224 | tf_op jit(solution)/shard_map/ppermute | solution.py:17
  12.1 96.6 %collective-permute-start = (f32[1,256,128]{2,1,0:T(8,128)S(1)}, f32[1,256,128]{2,1,0:T(8,128)S(1)}, u32[]{:S(2)}, u32[]{:S(2)}) collective-permute-start(f32[1,256,128]{2,1,0:T(8,128)S(1)} %get-tuple-element.12), channel_id=1, source_target_pairs={{8,0},{16,8},{24,16},{32,24},{40,32},{48,40},{56,48},{64,56},{72,6... | collective-permute-start | bytes 393224 | tf_op jit(solution)/shard_map/ppermute | solution.py:20
  32.3 72.8 %copy-start.3 = (f32[1,4,128,128]{3,2,1,0:T(8,128)S(1)}, f32[1,4,128,128]{3,2,1,0:T(8,128)}, u32[]{:S(2)}) copy-start(f32[1,4,128,128]{3,2,1,0:T(8,128)} %param.7) | copy-start | bytes 786436
  32.3 78.3 %copy-start.1 = (f32[128,128]{1,0:T(8,128)S(1)}, f32[128,128]{1,0:T(8,128)}, u32[]{:S(2)}) copy-start(f32[128,128]{1,0:T(8,128)} %param.9) | copy-start | bytes 196612
  105.6 5.0 %collective-permute-start.4 = (f32[1,128,128]{2,1,0:T(8,128)S(1)}, f32[1,128,128]{2,1,0:T(8,128)S(1)}, u32[]{:S(2)}, u32[]{:S(2)}) collective-permute-start(f32[1,128,128]{2,1,0:T(8,128)S(1)} %slice.129), channel_id=1, source_target_pairs={{0,8},{8,16},{16,24},{24,32},{32,40},{40,48},{48,56},{56,64},{64,7... | collective-permute-start | bytes 196616 | tf_op jit(solution)/shard_map/ppermute | solution.py:28
  111.0 11.0 %collective-permute-start.5 = (f32[1,128,128]{2,1,0:T(8,128)S(1)}, f32[1,128,128]{2,1,0:T(8,128)S(1)}, u32[]{:S(2)}, u32[]{:S(2)}) collective-permute-start(f32[1,128,128]{2,1,0:T(8,128)S(1)} %slice.133), channel_id=1, source_target_pairs={{0,8},{8,16},{16,24},{24,32},{32,40},{40,48},{48,56},{56,64},{64,7... | collective-permute-start | bytes 196616 | tf_op jit(solution)/shard_map/ppermute | solution.py:28
  116.3 9.3 %collective-permute-start.3 = (f32[66,1,128]{2,1,0:T(1,128)S(1)}, f32[66,1,128]{2,1,0:T(1,128)S(1)}, u32[]{:S(2)}, u32[]{:S(2)}) collective-permute-start(f32[66,1,128]{2,1,0:T(1,128)S(1)} %get-tuple-element.11), channel_id=1, source_target_pairs={{0,1},{1,2},{2,3},{3,4},{4,5},{5,6},{6,7},{8,9},{9,10},{10,11},{11... | collective-permute-start | bytes 101384 | tf_op jit(solution)/shard_map/ppermute | solution.py:17
  118.3 7.4 %collective-permute-start.2 = (f32[66,1,128]{2,1,0:T(1,128)S(1)}, f32[66,1,128]{2,1,0:T(1,128)S(1)}, u32[]{:S(2)}, u32[]{:S(2)}) collective-permute-start(f32[66,1,128]{2,1,0:T(1,128)S(1)} %get-tuple-element.10), channel_id=1, source_target_pairs={{1,0},{2,1},{3,2},{4,3},{5,4},{6,5},{7,6},{9,8},{10,9},{11,10},{12... | collective-permute-start | bytes 101384 | tf_op jit(solution)/shard_map/ppermute | solution.py:20
  122.4 45.0 %collective-permute-start.6 = (f32[1,128,128]{2,1,0:T(8,128)S(1)}, f32[1,128,128]{2,1,0:T(8,128)S(1)}, u32[]{:S(2)}, u32[]{:S(2)}) collective-permute-start(f32[1,128,128]{2,1,0:T(8,128)S(1)} %slice.136), channel_id=1, source_target_pairs={{0,8},{8,16},{16,24},{24,32},{32,40},{40,48},{48,56},{56,64},{64,7... | collective-permute-start | bytes 196616 | tf_op jit(solution)/shard_map/ppermute | solution.py:28
  167.7 42.2 %copy-start.2 = (f32[4,128,128]{2,1,0:T(8,128)}, f32[4,128,128]{2,1,0:T(8,128)S(1)}, u32[]{:S(2)}) copy-start(f32[4,128,128]{2,1,0:T(8,128)S(1)} %convolution_add_fusion) | copy-start | bytes 786436
Sparse Core Ops, SparseCore 0:
  24.9 76.8 reduce-scatter.3
where the time goes:
time: 217 us
  waiting for transfers between devices  63 us (29%)
  local copies, waits for them, and re-layouts  35.4 us (16%)
  matrix products  29 us (13%)
  blocking collectives  25.4 us (12%)
  other arithmetic  24.7 us (11%)
  starting transfers between devices  21.3 us (10%)
  between operations  17.9 us (8%)
    unnamed x2, waiting for transfers between devices  61.8 us
    dot_general x1, matrix products, shards(): mixed = jnp.einsum('xyc,cd->xyd', parent, parent_mix, precision=HIGH)  27 us
    all_gather x1, blocking collectives, shards(): piece = lax.all_gather(own_values, 'tiles', axis=0, tiled=True)  25.4 us
    unnamed x4, other arithmetic  15.1 us
    gather x2, local copies, waits for them, and re-layouts, shards(): parent_new[jnp.clip(prow, 0, tile_rows - 1)[:, None], jnp.clip(pcol, 0, t...  14.5 us
    ppermute x3, starting transfers between devices, passed_along(): return lax.ppermute(block, axis, route)  10.6 us
    unnamed x17, local copies, waits for them, and re-layouts  8.47 us
    ppermute x2, starting transfers between devices, with_halo(): lax.ppermute(lax.slice_in_dim(block, block.shape[dim] - width, None, axis...  5.75 us
  transfers between devices with their start and end apart: 8, of which 2 were waited for; matrix products, arithmetic and copies ran while one was open for 33% of the time, Pallas kernels for 0%

commit v1 on v0

--- a/solution.py
+++ b/solution.py
@@ -100,7 +100,10 @@
     own_values = jnp.where((row_live[:, None] & col_live[None, :])[..., None], own_values, 0.0)
     pcol = (anchor[1] + ys) // 3 - column_index * tile_cols
     col_ok = col_live & (pcol >= 0) & (pcol < tile_cols)
-    piece = lax.all_gather(own_values, "tiles", axis=0, tiled=True)
+    size = lax.axis_size("tiles")
+    blocks = jnp.stack([own_values for _ in range(size)])
+    blocks = lax.all_to_all(blocks, "tiles", split_axis=0, concat_axis=0)
+    piece = jnp.concatenate(blocks, axis=0)
     slot_index = jnp.arange(piece.shape[0], dtype=jnp.int32)
     sender = slot_index // fb_rows
     sender_base = sender * nest_rows

time: 217 us -> 210 us (0.968)
  blocking collectives: 25.4 us -> 0 us
  waiting for transfers between devices: 63 us -> 70.5 us
  starting transfers between devices: 21.3 us -> 28.6 us
    all_gather x1 -> x0, blocking collectives: 25.4 us -> none  [shards(): piece = lax.all_gather(own_values, 'tiles', axis=0, tiled=True)]
    unnamed x2, waiting for transfers between devices: 61.8 us -> 69.3 us
    all_to_all x0 -> x1, starting transfers between devices: none -> 7.09 us  [shards(): blocks = lax.all_to_all(blocks, 'tiles', split_axis=0, concat_axis=0)]
  transfers between devices with their start and end apart: 8 -> 9, of which waited for: 2 -> 2; matrix products, arithmetic and copies ran while one was open for 33% -> 36% of each run, Pallas kernels for 0% -> 0%
where the time goes in v1:
time: 210 us; the launch traced here: 208 us
  waiting for transfers between devices  70.5 us (34%)
  local copies, waits for them, and re-layouts  36.7 us (17%)
  matrix products  29 us (14%)
  starting transfers between devices  28.6 us (14%)
  other arithmetic  24.9 us (12%)
  between operations  18.1 us (9%)
    unnamed x2, waiting for transfers between devices  69.3 us
    dot_general x1, matrix products, shards(): mixed = jnp.einsum('xyc,cd->xyd', parent, parent_mix, precision=HIGH)  27 us
    unnamed x4, other arithmetic  15.1 us
    gather x2, local copies, waits for them, and re-layouts, shards(): parent_new[jnp.clip(prow, 0, tile_rows - 1)[:, None], jnp.clip(pcol, 0, t...  14.5 us
    ppermute x3, starting transfers between devices, passed_along(): return lax.ppermute(block, axis, route)  10.7 us
    unnamed x17, local copies, waits for them, and re-layouts  8.47 us
    all_to_all x1, starting transfers between devices, shards(): blocks = lax.all_to_all(blocks, 'tiles', split_axis=0, concat_axis=0)  7.09 us
    ppermute x2, starting transfers between devices, with_halo(): lax.ppermute(lax.slice_in_dim(block, block.shape[dim] - width, None, axis...  5.75 us
  transfers between devices with their start and end apart: 9, of which 2 were waited for; matrix products, arithmetic and copies ran while one was open for 36% of the time, Pallas kernels for 0%

profile of v1, /device:TPU:6, one launch (start us, length us, event | category | flops | bytes accessed | tf_op | source)
XLA Modules:
  0.0 207.7 jit_solution(4750958470445217293)
XLA Ops:
  7.3 1.1 fusion.73
  8.3 3.8 %collective-permute-start.1 = (f32[1,256,128]{2,1,0:T(8,128)S(1)}, f32[1,256,128]{2,1,0:T(8,128)S(1)}, u32[]{:S(2)}, u32[]{:S(2)}) collective-permute-start(f32[1,256,128]{2,1,0:T(8,128)S(1)} %get-tuple-element.13), channel_id=1, source_target_pairs={{0,8},{8,16},{16,24},{24,32},{32,40},{40,48},{48,56},{56,64},{64,7... | collective-permute-start | bytes 393224 | tf_op jit(solution)/shard_map/ppermute | solution.py:17
  12.2 1.3 collective-permute-start
  13.5 1.4 fusion.74
  18.5 2.0 constant_dynamic-slice_fusion
  20.6 1.8 gather_fusion
  22.4 2.7 %broadcast_select_fusion = f32[16,3,64,128]{3,2,1,0:T(8,128)} fusion(f32[16,3,64,128]{3,2,1,0:T(8,128)} %bitcast.66, pred[16,3]{1,0:T(8,128)(4,1)S(1)} %fusion.46), kind=kLoop, calls=%fused_computation.30 | loop fusion | flops 393216 | bytes 3145776 | tf_op jit(solution)/shard_map/jit(_where)/select_n | solution.py:73
  25.1 0.7 clamp_shift-left_fusion
  32.9 69.2 %reduce-scatter.4.cloned.1.call-done = f32[1,3,64,128]{3,2,1,0:T(8,128)} async-done(((f32[16,3,64,128]{3,2,1,0:T(8,128)}), f32[1,3,64,128]{3,2,1,0:T(8,128)}) %reduce-scatter.4.cloned.1.call-update) | async-done | bytes 98320
  102.1 1.4 gather_fusion.1
  103.6 1.4 gather_fusion.2
  105.9 3.2 %collective-permute-start.4 = (f32[1,128,128]{2,1,0:T(8,128)S(1)}, f32[1,128,128]{2,1,0:T(8,128)S(1)}, u32[]{:S(2)}, u32[]{:S(2)}) collective-permute-start(f32[1,128,128]{2,1,0:T(8,128)S(1)} %slice.129), channel_id=1, source_target_pairs={{0,8},{8,16},{16,24},{24,32},{32,40},{40,48},{48,56},{56,64},{64,7... | collective-permute-start | bytes 196616 | tf_op jit(solution)/shard_map/ppermute | solution.py:28
  109.1 7.7 %constant_dynamic-update-slice_fusion.1 = f32[66,256,128]{2,1,0:T(8,128)} fusion(f32[66,256,128]{2,1,0:T(8,128)} %constant_dynamic-update-slice_fusion.2, f32[64,256,128]{2,1,0:T(8,128)} %param.6), kind=kLoop, calls=%fused_computation.90 | loop fusion | bytes 16777216
  117.2 3.3 %collective-permute-start.5 = (f32[1,128,128]{2,1,0:T(8,128)S(1)}, f32[1,128,128]{2,1,0:T(8,128)S(1)}, u32[]{:S(2)}, u32[]{:S(2)}) collective-permute-start(f32[1,128,128]{2,1,0:T(8,128)S(1)} %slice.133), channel_id=1, source_target_pairs={{0,8},{8,16},{16,24},{24,32},{32,40},{40,48},{48,56},{56,64},{64,7... | collective-permute-start | bytes 196616 | tf_op jit(solution)/shard_map/ppermute | solution.py:28
  121.2 1.2 collective-permute-done.5
  122.8 4.3 %collective-permute-start.6 = (f32[1,128,128]{2,1,0:T(8,128)S(1)}, f32[1,128,128]{2,1,0:T(8,128)S(1)}, u32[]{:S(2)}, u32[]{:S(2)}) collective-permute-start(f32[1,128,128]{2,1,0:T(8,128)S(1)} %slice.136), channel_id=1, source_target_pairs={{0,8},{8,16},{16,24},{24,32},{32,40},{40,48},{48,56},{56,64},{64,7... | collective-permute-start | bytes 196616 | tf_op jit(solution)/shard_map/ppermute | solution.py:28
  127.1 1.1 fusion.72
  128.2 1.9 collective-permute-start.3
  130.1 3.6 %collective-permute-start.2 = (f32[66,1,128]{2,1,0:T(1,128)S(1)}, f32[66,1,128]{2,1,0:T(1,128)S(1)}, u32[]{:S(2)}, u32[]{:S(2)}) collective-permute-start(f32[66,1,128]{2,1,0:T(1,128)S(1)} %get-tuple-element.10), channel_id=1, source_target_pairs={{1,0},{2,1},{3,2},{4,3},{5,4},{6,5},{7,6},{9,8},{10,9},{11,10},{12... | collective-permute-start | bytes 101384 | tf_op jit(solution)/shard_map/ppermute | solution.py:20
  135.6 1.1 stack.2
  136.7 7.1 %all-to-all-start = ((f32[16,2,43,128]{3,1,2,0:T(2,128)}), f32[16,2,43,128]{3,1,2,0:T(2,128)S(1)}, u32[]{:S(2)}, u32[]{:S(2)}) async-start(f32[16,2,43,128]{3,1,2,0:T(2,128)} %stack.2), calls=%async_computation | async-start | bytes 1409024 | tf_op jit(solution)/shard_map/all_to_all | solution.py:105
  143.9 27.0 %fusion.4 = f32[64,256,128]{2,1,0:T(8,128)} fusion(f32[64,256,128]{2,1,0:T(8,128)} %param.6, f32[66,256,128]{2,1,0:T(8,128)} %constant_dynamic-update-slice_fusion, f32[66,1,128]{2,1,0:T(1,128)S(1)} %collective-permute-done.3, f32[66,1,128]{2,1,0:T(1,128)S(1)} %collective-permute-done.2, f32[1,256,128]{2,1,0:T(8,128)S(1)} %collective-permute-done.1, ...), kind=kOutput, calls=%fused_computation.12 | convolution fusion | flops 3246391296 | bytes 25823232 | tf_op jit(solution)/shard_map/xyc,cd->xyd/dot_general | solution.py:77
  170.9 14.5 %gather_fusion.5 = f32[1376,128]{1,0:T(8,128)S(1)} fusion(f32[64,256,128]{2,1,0:T(8,128)} %fusion.4, s32[1376]{0:T(1024)S(1)} %reshape.577), kind=kCustom, calls=%fused_computation.5 | custom fusion | bytes 1420032 | tf_op jit(solution)/shard_map/gather | solution.py:114
  185.9 14.9 %scatter_fusion = f32[16384,128]{1,0:T(8,128)} fusion(f32[16384,128]{1,0:T(8,128)} %bitcast.64, s32[1376]{0:T(1024)S(1)} %reshape.583, f32[1376,128]{1,0:T(8,128)S(1)} %reshape.585), kind=kCustom, calls=%fused_computation.6 | custom fusion | flops 176128 | bytes 2119040
  (80 shorter events, 11.8 us)
Async XLA Ops:
  7.2 136.7 %copy-start = (f32[128,128]{1,0:T(8,128)S(1)}, f32[128,128]{1,0:T(8,128)}, u32[]{:S(2)}) copy-start(f32[128,128]{1,0:T(8,128)} %param.8) | copy-start | bytes 196612
  7.2 24.4 %copy-start.6 = (s32[2]{0:T(128)S(1)}, s32[2]{0:T(128)}, u32[]{:S(2)}) copy-start(s32[2]{0:T(128)} %constant.162) | copy-start | bytes 28
  7.2 24.4 %copy-start.5 = (s32[2]{0:T(128)S(1)}, s32[2]{0:T(128)}, u32[]{:S(2)}) copy-start(s32[2]{0:T(128)} %constant.165) | copy-start | bytes 28
  7.2 24.5 %copy-start.4 = (f32[2,128]{1,0:T(2,128)S(1)}, f32[2,128]{1,0:T(2,128)}, u32[]{:S(2)}) copy-start(f32[2,128]{1,0:T(2,128)} %param.10) | copy-start | bytes 3076
  7.2 98.2 %copy-start.3 = (f32[1,4,128,128]{3,2,1,0:T(8,128)S(1)}, f32[1,4,128,128]{3,2,1,0:T(8,128)}, u32[]{:S(2)}) copy-start(f32[1,4,128,128]{3,2,1,0:T(8,128)} %param.7) | copy-start | bytes 786436
  7.2 94.9 %reduce-scatter.4.cloned.1.call-start = ((), (), s32[]{:S(2)}) async-start(), calls=%async_computation.2 | async-start | bytes 1671168
  8.3 23.9 %collective-permute-start.1 = (f32[1,256,128]{2,1,0:T(8,128)S(1)}, f32[1,256,128]{2,1,0:T(8,128)S(1)}, u32[]{:S(2)}, u32[]{:S(2)}) collective-permute-start(f32[1,256,128]{2,1,0:T(8,128)S(1)} %get-tuple-element.13), channel_id=1, source_target_pairs={{0,8},{8,16},{16,24},{24,32},{32,40},{40,48},{48,56},{56,64},{64,7... | collective-permute-start | bytes 393224 | tf_op jit(solution)/shard_map/ppermute | solution.py:17
  12.2 108.4 %collective-permute-start = (f32[1,256,128]{2,1,0:T(8,128)S(1)}, f32[1,256,128]{2,1,0:T(8,128)S(1)}, u32[]{:S(2)}, u32[]{:S(2)}) collective-permute-start(f32[1,256,128]{2,1,0:T(8,128)S(1)} %get-tuple-element.12), channel_id=1, source_target_pairs={{8,0},{16,8},{24,16},{32,24},{40,32},{48,40},{56,48},{64,56},{72,6... | collective-permute-start | bytes 393224 | tf_op jit(solution)/shard_map/ppermute | solution.py:20
  105.9 10.9 %copy-start.1 = (f32[128,128]{1,0:T(8,128)S(1)}, f32[128,128]{1,0:T(8,128)}, u32[]{:S(2)}) copy-start(f32[128,128]{1,0:T(8,128)} %param.9) | copy-start | bytes 196612
  105.9 10.9 %collective-permute-start.4 = (f32[1,128,128]{2,1,0:T(8,128)S(1)}, f32[1,128,128]{2,1,0:T(8,128)S(1)}, u32[]{:S(2)}, u32[]{:S(2)}) collective-permute-start(f32[1,128,128]{2,1,0:T(8,128)S(1)} %slice.129), channel_id=1, source_target_pairs={{0,8},{8,16},{16,24},{24,32},{32,40},{40,48},{48,56},{56,64},{64,7... | collective-permute-start | bytes 196616 | tf_op jit(solution)/shard_map/ppermute | solution.py:28
  117.2 5.2 %collective-permute-start.5 = (f32[1,128,128]{2,1,0:T(8,128)S(1)}, f32[1,128,128]{2,1,0:T(8,128)S(1)}, u32[]{:S(2)}, u32[]{:S(2)}) collective-permute-start(f32[1,128,128]{2,1,0:T(8,128)S(1)} %slice.133), channel_id=1, source_target_pairs={{0,8},{8,16},{16,24},{24,32},{32,40},{40,48},{48,56},{56,64},{64,7... | collective-permute-start | bytes 196616 | tf_op jit(solution)/shard_map/ppermute | solution.py:28
  122.8 11.0 %collective-permute-start.6 = (f32[1,128,128]{2,1,0:T(8,128)S(1)}, f32[1,128,128]{2,1,0:T(8,128)S(1)}, u32[]{:S(2)}, u32[]{:S(2)}) collective-permute-start(f32[1,128,128]{2,1,0:T(8,128)S(1)} %slice.136), channel_id=1, source_target_pairs={{0,8},{8,16},{16,24},{24,32},{32,40},{40,48},{48,56},{56,64},{64,7... | collective-permute-start | bytes 196616 | tf_op jit(solution)/shard_map/ppermute | solution.py:28
  128.2 15.6 %collective-permute-start.3 = (f32[66,1,128]{2,1,0:T(1,128)S(1)}, f32[66,1,128]{2,1,0:T(1,128)S(1)}, u32[]{:S(2)}, u32[]{:S(2)}) collective-permute-start(f32[66,1,128]{2,1,0:T(1,128)S(1)} %get-tuple-element.11), channel_id=1, source_target_pairs={{0,1},{1,2},{2,3},{3,4},{4,5},{5,6},{6,7},{8,9},{9,10},{10,11},{11... | collective-permute-start | bytes 101384 | tf_op jit(solution)/shard_map/ppermute | solution.py:17
  130.1 13.7 %collective-permute-start.2 = (f32[66,1,128]{2,1,0:T(1,128)S(1)}, f32[66,1,128]{2,1,0:T(1,128)S(1)}, u32[]{:S(2)}, u32[]{:S(2)}) collective-permute-start(f32[66,1,128]{2,1,0:T(1,128)S(1)} %get-tuple-element.10), channel_id=1, source_target_pairs={{1,0},{2,1},{3,2},{4,3},{5,4},{6,5},{7,6},{9,8},{10,9},{11,10},{12... | collective-permute-start | bytes 101384 | tf_op jit(solution)/shard_map/ppermute | solution.py:20
  134.2 36.7 %copy-start.2 = (f32[4,128,128]{2,1,0:T(8,128)}, f32[4,128,128]{2,1,0:T(8,128)S(1)}, u32[]{:S(2)}) copy-start(f32[4,128,128]{2,1,0:T(8,128)S(1)} %convolution_add_fusion) | copy-start | bytes 786436
  136.7 48.7 %all-to-all-start = ((f32[16,2,43,128]{3,1,2,0:T(2,128)}), f32[16,2,43,128]{3,1,2,0:T(2,128)S(1)}, u32[]{:S(2)}, u32[]{:S(2)}) async-start(f32[16,2,43,128]{3,1,2,0:T(2,128)} %stack.2), calls=%async_computation | async-start | bytes 1409024 | tf_op jit(solution)/shard_map/all_to_all | solution.py:105
Sparse Core Ops, SparseCore 0:
  25.3 76.8 reduce-scatter.3
